TPU v7x, 256 devices: a whole 4x4x8 slice. The times are simulated.
256 devices in a mesh: lat: 8 (over z), lon: 16 (over x, y), mem: 2 (over core).
Axes of the slice: x: 4, y: 4, z: 8, core: 2. Of those that a mesh axis runs over, the one named last changes fastest.
Arguments:
- measured_inputs: bfloat16 [4096, 128, 256], P(('lat', 'lon', 'mem')), may hold values from -6 to 6
- target_sector: int32 [4096], P(('lat', 'lon', 'mem')), may hold values from 0 to 15, as said below
- hidden_member_fields: bfloat16 [2, 64, 128, 768], P('mem', 'lat', 'lon'), may hold values from -6 to 6
- analysis_adjoint: bfloat16 [2, 64, 128, 768], P('mem', 'lat', 'lon'), may hold values from -0.29882812 to 0.29882812
- inner_perceptron_coeffs: bfloat16 [256, 256], replicated, may hold values from -0.375 to 0.375
- outer_perceptron_coeffs: bfloat16 [256, 768], replicated, may hold values from -0.375 to 0.375
- probe_projector: bfloat16 [768, 768], replicated, may hold values from -0.21875 to 0.21875
- logit_sharpness: float32 [12], replicated, may hold values from 0.5 to 2.5
- adjacent_channel_coeffs: float32 [8, 768], replicated, may hold values from -0.7 to 0.7
Outputs:
- analysis: bfloat16 [2, 64, 128, 768], P('mem', 'lat', 'lon')
- in_weight_grad: float32 [256, 256], replicated
- out_weight_grad: float32 [256, 768], replicated
Inputs may be any that keep to these rules, and one draw needn't show every extreme that they name: `target_sector`: of the 16 blocks of one device at most 2 have one destination, and one destination has exactly 2; in every band and member one sector receives exactly 2 blocks from every device of the band, 32 in all, and no sector receives more.
All inputs are finite; a program needn't handle non-finite values.
Results may differ from a plain program's by a relative error of at most 0.012.
The roundings to bfloat16 on the way count: a program that leaves them out, or rounds other values in their place, can miss the bound.
Values may be sent and summed in bfloat16 or wider, within the bound.
No kernel may reach another device: no remote copies, remote signals or barrier semaphores. Data moves between devices by JAX's collectives and lax.ppermute only.
A program may use at most 192 MiB of HBM per device.

v0:
```python
import math

import jax
import jax.numpy as jnp
from jax import lax
from jax.sharding import PartitionSpec as P

HEADS = 12
CHANNELS_PER_ATT = 64


NEIGHBOURS = ((-1, -1), (-1, 0), (-1, 1), (0, -1), (0, 1), (1, -1), (1, 0), (1, 1))


def extended(block, sides, width):
    for axis, dim in sides:
        count = lax.axis_size(axis)
        forward = [(i, i + 1) for i in range(count - 1)]
        forward.append((count - 1, 0))
        backward = [(target, source) for source, target in forward]
        low = lax.ppermute(
            lax.slice_in_dim(block, block.shape[dim] - width, None, axis=dim), axis, forward
        )
        high = lax.ppermute(lax.slice_in_dim(block, 0, width, axis=dim), axis, backward)
        block = jnp.concatenate([low, block, high], axis=dim)
    return block


def silu_slope(pre_act):
    sigmoid_val = jax.nn.sigmoid(pre_act)
    return sigmoid_val * (1.0 + pre_act * (1.0 - sigmoid_val))


def mix_local(padded, keep_rows, adjacent_channel_coeffs, direction):
    values = padded.astype(jnp.float32) * keep_rows[:, None, None]
    n_rows = padded.shape[0] - 2
    n_cols = padded.shape[1] - 2
    total = values[1 : 1 + n_rows, 1 : 1 + n_cols]
    for offset_idx, (row_step, col_step) in enumerate(NEIGHBOURS):
        row_start = 1 + direction * row_step
        col_start = 1 + direction * col_step
        total = (
            total
            + adjacent_channel_coeffs[offset_idx]
            * values[row_start : row_start + n_rows, col_start : col_start + n_cols]
        )
    return total


def mutual_attention_apply(
    probe_projection,
    grid_point_entries,
    lookup_projection_entries,
    genuine_entry_indicator,
    logit_sharpness,
):
    n_cells = grid_point_entries.shape[0]
    n_tokens = lookup_projection_entries.shape[0]
    query_heads = probe_projection.reshape(n_cells, HEADS, CHANNELS_PER_ATT)
    key_heads = lookup_projection_entries.reshape(n_tokens, HEADS, CHANNELS_PER_ATT)
    latent_heads = grid_point_entries.reshape(n_cells, HEADS, CHANNELS_PER_ATT)
    normaliser_entries = logit_sharpness / math.sqrt(CHANNELS_PER_ATT)
    scores = jnp.einsum("qhd,khd->hqk", query_heads, key_heads, preferred_element_type=jnp.float32)
    scores = jnp.where(
        genuine_entry_indicator[None, None, :], scores * normaliser_entries[:, None, None], -jnp.inf
    )
    self_score = jnp.einsum(
        "qhd,qhd->hq", query_heads, latent_heads, preferred_element_type=jnp.float32
    )
    self_score = self_score * normaliser_entries[:, None]
    row_max = jnp.maximum(jnp.max(scores, axis=2), self_score)
    exp_terms = jnp.exp(scores - row_max[:, :, None])
    self_exp = jnp.exp(self_score - row_max)
    denominator = jnp.sum(exp_terms, axis=2) + self_exp
    probs = exp_terms / denominator[:, :, None]
    self_prob = self_exp / denominator
    weights = probs.astype(jnp.bfloat16)
    self_weight = lax.optimization_barrier(self_prob.astype(jnp.bfloat16)).astype(jnp.float32)
    update = jnp.einsum("hqk,khd->qhd", weights, key_heads, preferred_element_type=jnp.float32)
    update = update + jnp.transpose(self_weight)[:, :, None] * latent_heads.astype(jnp.float32)
    revised_analysis = (
        grid_point_entries.astype(jnp.float32) + update.reshape(n_cells, HEADS * CHANNELS_PER_ATT)
    ).astype(jnp.bfloat16)
    return (revised_analysis, (probs, self_prob, weights))


def mutual_attention_adjoint(
    probe_projection,
    grid_point_entries,
    lookup_projection_entries,
    retained_intermediates,
    hidden_field_adjoint,
    logit_sharpness,
):
    probs, self_prob, weights = retained_intermediates
    n_cells = grid_point_entries.shape[0]
    n_tokens = lookup_projection_entries.shape[0]
    query_heads = probe_projection.reshape(n_cells, HEADS, CHANNELS_PER_ATT)
    key_heads = lookup_projection_entries.reshape(n_tokens, HEADS, CHANNELS_PER_ATT)
    latent_heads = grid_point_entries.reshape(n_cells, HEADS, CHANNELS_PER_ATT)
    grad_heads = hidden_field_adjoint.reshape(n_cells, HEADS, CHANNELS_PER_ATT)
    normaliser_entries = logit_sharpness / math.sqrt(CHANNELS_PER_ATT)
    weight_grad = jnp.einsum(
        "qhd,khd->hqk", grad_heads, key_heads, preferred_element_type=jnp.float32
    )
    self_grad = jnp.einsum(
        "qhd,qhd->hq", grad_heads, latent_heads, preferred_element_type=jnp.float32
    )
    row_total = jnp.sum(probs * weight_grad, axis=2) + self_prob * self_grad
    logit_grad = (
        probs * (weight_grad - row_total[:, :, None]) * normaliser_entries[:, None, None]
    ).astype(jnp.bfloat16)
    measured_embedding_adjoint = jnp.einsum(
        "hqk,qhd->khd", weights, grad_heads, preferred_element_type=jnp.float32
    )
    measured_embedding_adjoint = measured_embedding_adjoint + jnp.einsum(
        "hqk,qhd->khd", logit_grad, query_heads, preferred_element_type=jnp.float32
    )
    return measured_embedding_adjoint.reshape(n_tokens, HEADS * CHANNELS_PER_ATT).astype(
        jnp.bfloat16
    )


def per_device(
    measured_inputs,
    target_sector,
    hidden_member_fields,
    analysis_adjoint,
    inner_perceptron_coeffs,
    outer_perceptron_coeffs,
    probe_projector,
    logit_sharpness,
    adjacent_channel_coeffs,
):
    lon_count = lax.axis_size("lon")
    lat_count = lax.axis_size("lat")
    block_count = target_sector.shape[0]
    block_len = measured_inputs.shape[1]
    obs_width = measured_inputs.shape[2]
    model_width = hidden_member_fields.shape[3]
    hidden_width = inner_perceptron_coeffs.shape[1]
    cell_rows = hidden_member_fields.shape[1]
    cell_cols = hidden_member_fields.shape[2]
    n_cells = cell_rows * cell_cols
    cap_slots = max(2, 2 * block_count // lon_count)
    sector_ids = jnp.arange(lon_count, dtype=jnp.int32)
    one_hot = (target_sector[:, None] == sector_ids[None, :]).astype(jnp.int32)
    earlier = jnp.cumsum(one_hot, axis=0) - one_hot
    slot_index = target_sector * cap_slots + jnp.sum(earlier * one_hot, axis=1)
    cot_padded = extended(analysis_adjoint[0], (("lat", 0), ("lon", 1)), 1)
    band_targets = lax.all_gather(target_sector, "lon", axis=0, tiled=True)
    own_sector = lax.axis_index("lon")
    arrivals = jnp.sum(
        (band_targets == own_sector).astype(jnp.int32).reshape(lon_count, block_count), axis=1
    )
    live_slots = jnp.arange(cap_slots, dtype=jnp.int32)[None, :] < arrivals[:, None]
    genuine_entry_indicator = jnp.broadcast_to(
        live_slots[:, :, None], (lon_count, cap_slots, block_len)
    ).reshape(-1)
    grid_point_entries = hidden_member_fields.reshape(n_cells, model_width)
    probe_projection = jnp.dot(
        grid_point_entries, probe_projector, preferred_element_type=jnp.float32
    ).astype(jnp.bfloat16)
    send_blocks = jnp.zeros((lon_count * cap_slots, block_len, obs_width), jnp.bfloat16)
    send_blocks = (
        send_blocks.at[slot_index]
        .set(measured_inputs)
        .reshape(lon_count, cap_slots, block_len, obs_width)
    )
    obs_blocks = lax.all_to_all(send_blocks, "lon", split_axis=0, concat_axis=0, tiled=True)
    pre_act = jnp.dot(obs_blocks, inner_perceptron_coeffs, preferred_element_type=jnp.float32)
    hidden_act = jax.nn.silu(pre_act).astype(jnp.bfloat16)
    obs_feat = jnp.dot(
        hidden_act, outer_perceptron_coeffs, preferred_element_type=jnp.float32
    ).astype(jnp.bfloat16)
    token_blocks, pre_act, hidden_act, obs_feat = (obs_blocks, pre_act, hidden_act, obs_feat)
    lookup_projection_entries = obs_feat.reshape(-1, model_width)
    revised_analysis, retained_intermediates = mutual_attention_apply(
        probe_projection,
        grid_point_entries,
        lookup_projection_entries,
        genuine_entry_indicator,
        logit_sharpness,
    )
    state_grid = revised_analysis.reshape(cell_rows, cell_cols, model_width)
    state_padded = extended(state_grid, (("lat", 0), ("lon", 1)), 1)
    lat_index = lax.axis_index("lat")
    keep_rows = jnp.ones((cell_rows + 2,), jnp.float32)
    keep_rows = keep_rows.at[0].set(jnp.where(lat_index > 0, 1.0, 0.0))
    keep_rows = keep_rows.at[cell_rows + 1].set(jnp.where(lat_index < lat_count - 1, 1.0, 0.0))
    analysis = (
        mix_local(state_padded, keep_rows, adjacent_channel_coeffs, 1)
        .astype(jnp.bfloat16)
        .reshape(hidden_member_fields.shape)
    )
    hidden_field_adjoint = (
        mix_local(cot_padded, keep_rows, adjacent_channel_coeffs, -1)
        .astype(jnp.bfloat16)
        .reshape(n_cells, model_width)
    )
    measured_embedding_adjoint = mutual_attention_adjoint(
        probe_projection,
        grid_point_entries,
        lookup_projection_entries,
        retained_intermediates,
        hidden_field_adjoint,
        logit_sharpness,
    )
    grad_blocks = measured_embedding_adjoint.reshape(lon_count, cap_slots, block_len, model_width)
    grad_rows = grad_blocks.reshape(-1, model_width)
    hidden_rows = hidden_act.reshape(-1, hidden_width)
    pre_rows = pre_act.reshape(-1, hidden_width)
    hidden_grad = jnp.einsum(
        "td,hd->th", grad_rows, outer_perceptron_coeffs, preferred_element_type=jnp.float32
    )
    hidden_grad = (hidden_grad * silu_slope(pre_rows)).astype(jnp.bfloat16)
    out_grad = jnp.einsum("th,td->hd", hidden_rows, grad_rows, preferred_element_type=jnp.float32)
    in_grad = jnp.einsum(
        "tc,th->ch",
        token_blocks.reshape(-1, obs_width),
        hidden_grad,
        preferred_element_type=jnp.float32,
    )
    in_grad, out_grad = lax.psum((in_grad, out_grad), ("lat", "lon", "mem"))
    return (analysis, in_grad, out_grad)


def solution(mesh):
    in_specs = (
        P(("lat", "lon", "mem"), None, None),
        P(("lat", "lon", "mem")),
        P("mem", "lat", "lon", None),
        P("mem", "lat", "lon", None),
        P(),
        P(),
        P(),
        P(),
        P(),
    )
    out_specs = (P("mem", "lat", "lon", None), P(), P())
    return jax.shard_map(
        per_device, mesh=mesh, in_specs=in_specs, out_specs=out_specs, check_vma=False
    )
```

profile of v0, /device:TPU:2, one launch (start us, length us, event | category | flops | bytes accessed | tf_op | source)
XLA Modules:
  0.0 453.2 jit_solution(17303583192215351556)
XLA Ops:
  11.2 3.4 scatter_fusion
  14.6 7.5 %all-to-all-start = ((bf16[16,2,128,256]{3,2,1,0:T(8,128)(2,1)}), bf16[16,2,128,256]{3,2,1,0:T(8,128)(2,1)S(1)}, u32[]{:S(2)}, u32[]{:S(2)}) async-start(bf16[16,2,128,256]{3,2,1,0:T(8,128)(2,1)} %bitcast.5), calls=%async_computation | async-start | bytes 4194304 | tf_op jit(solution)/shard_map/all_to_all | solution.py:170
  22.1 6.0 %collective-permute-start.5 = (bf16[1,8,768]{2,1,0:T(8,128)(2,1)S(1)}, bf16[1,8,768]{2,1,0:T(8,128)(2,1)S(1)}, u32[]{:S(2)}, u32[]{:S(2)}) collective-permute-start(bf16[1,8,768]{2,1,0:T(8,128)(2,1)S(1)} %get-tuple-element.48), channel_id=1, source_target_pairs={{32,0},{64,32},{96,64},{128,96},{160,128},{192,160},{224,192},{0,2... | collective-permute-start | bytes 36872 | tf_op jit(solution)/shard_map/ppermute | solution.py:24
  29.6 22.9 %all-reduce.1 = s32[256]{0:T(256)S(1)} all-reduce(s32[256]{0:T(256)S(1)} %dynamic-update-slice.6), channel_id=1, replica_groups=mesh['lat'=8,'lon'=16,'mem'=2] {'lon'}, use_global_device_ids=true, to_apply=%add.1 | all-reduce | flops 256 | bytes 2048
  57.5 6.6 %collective-permute-start.7 = (bf16[10,1,768]{2,1,0:T(2,128)(2,1)S(1)}, bf16[10,1,768]{2,1,0:T(2,128)(2,1)S(1)}, u32[]{:S(2)}, u32[]{:S(2)}) collective-permute-start(bf16[10,1,768]{2,1,0:T(2,128)(2,1)S(1)} %get-tuple-element.44), channel_id=1, source_target_pairs={{2,0},{4,2},{6,4},{8,6},{10,8},{12,10},{14,12},{16,14},{18,16},{20... | collective-permute-start | bytes 46088 | tf_op jit(solution)/shard_map/ppermute | solution.py:24
  71.3 4.3 multiply_convert_fusion.2
  77.0 4.5 convolution_convert_fusion
  81.4 16.2 %copy.30 = bf16[16,2,128,768]{2,1,0,3:T(2,128)(2,1)} copy(bf16[16,2,128,768]{3,2,1,0:T(8,128)(2,1)} %convolution_convert_fusion) | data formatting | bytes 12582912 | tf_op jit(solution)/shard_map/convert_element_type | solution.py:175
  97.6 11.2 %reshape_reshape.11 = bf16[4096,12,64]{0,2,1:T(8,128)(2,1)} reshape(bf16[16,2,128,768]{2,1,0,3:T(2,128)(2,1)} %copy.30) | data formatting | bytes 12582912 | tf_op jit(solution)/shard_map/reshape;reshape | solution.py:60
  108.8 4.1 fusion
  113.1 3.1 fusion.2
  116.3 4.1 copy-done.3
  120.3 7.3 %multiply_reduce_fusion = (f32[12,64]{1,0:T(8,128)S(1)}, f32[12,64,4096]{2,1,0:T(8,128)}) fusion(f32[12,64]{1,0:T(8,128)S(1)} %fusion.53, f32[12,64]{1,0:T(8,128)S(1)} %multiply_maximum_fusion, f32[12,64,4096]{2,1,0:T(8,128)S(1)} %get-tuple-element.52, f32[12]{0:T(128)S(1)} %broadcast_multiply_fusion, pred[4096]{0:T(1024)(128)(4,1)S(1)} %broadcast_in_dim.23, ...), kind=kOutput, calls=%fused_computation.3 | convolution fusion | flops 421526784 | bytes 31568944 | tf_op jit(solution)/shard_map/qhd,khd->hqk/dot_general | solution.py:103
  127.6 6.7 %fusion.11 = f32[12,64,4096]{2,1,0:T(8,128)} fusion(bf16[64,12,64]{2,1,0:T(8,128)(2,1)S(1)} %copy-done.9, f32[12,64,4096]{2,1,0:T(8,128)S(1)} %get-tuple-element.52, f32[12,64]{1,0:T(8,128)S(1)} %fusion.53, f32[12,64]{1,0:T(8,128)S(1)} %multiply_maximum_fusion, f32[12]{0:T(128)S(1)} %broadcast_multiply_fusion, pred[4096]{0:T(1024)(128)(4,1)S(1)} %broadcast_in_dim.23), kind=kOutput, calls=%fused_computation.22 | convolution fusion | flops 418381824 | bytes 25274416 | tf_op jit(solution)/shard_map/hqk,qhd->khd/dot_general | solution.py:113
  134.5 6.4 %fusion.18 = f32[64,12,64]{0,2,1:T(8,128)S(1)} fusion(bf16[4096,12,64]{0,2,1:T(8,128)(2,1)} %reshape_reshape.11, bf16[64,12,64]{0,2,1:T(8,128)(2,1)S(1)} %copy-done.11, f32[64,12]{0,1:T(8,128)S(1)} %convert_bitcast_fusion, f32[12,64,4096]{2,1,0:T(8,128)S(1)} %get-tuple-element.52, f32[12,64]{1,0:T(8,128)S(1)} %fusion.53, ...), kind=kOutput, calls=%fused_computation.27 | convolution fusion | flops 418529280 | bytes 19182640 | tf_op jit(solution)/shard_map/hqk,khd->qhd/dot_general | solution.py:79
  142.9 6.1 %collective-permute-start.1 = (bf16[1,8,768]{2,1,0:T(8,128)(2,1)S(1)}, bf16[1,8,768]{2,1,0:T(8,128)(2,1)S(1)}, u32[]{:S(2)}, u32[]{:S(2)}) collective-permute-start(bf16[1,8,768]{2,1,0:T(8,128)(2,1)S(1)} %get-tuple-element.46), channel_id=1, source_target_pairs={{32,0},{64,32},{96,64},{128,96},{160,128},{192,160},{224,192},{0,2... | collective-permute-start | bytes 36872 | tf_op jit(solution)/shard_map/ppermute | solution.py:24
  149.9 5.5 %fusion.10 = f32[4096,256]{1,0:T(8,128)} fusion(f32[16,2,128,256]{3,2,1,0:T(8,128)} %get-tuple-element.50), kind=kLoop, calls=%fused_computation.19 | loop fusion | flops 7340032 | bytes 8388608 | tf_op jit(solution)/shard_map/mul | solution.py:31
  155.4 17.7 %add_convert_fusion = bf16[12,64,4096]{2,1,0:T(8,128)(2,1)} fusion(f32[12,64,4096]{2,1,0:T(8,128)} %fusion.11, bf16[64,12,64]{0,2,1:T(8,128)(2,1)S(1)} %copy-done.7, f32[12,64,4096]{2,1,0:T(8,128)} %get-tuple-element.54, f32[12,64]{1,0:T(8,128)S(1)} %get-tuple-element.39, f32[12]{0:T(128)S(1)} %broadcast_multiply_fusion, f32[12,64,4096]{2,1,0:T(8,128)} %copy-done.2, ...), kind=kOutput, calls=%fused_computation.1 | convolution fusion | flops 434110464 | bytes 44151856 | tf_op jit(solution)/shard_map/hqk,qhd->khd/dot_general | solution.py:116
  173.1 6.1 %fusion.58 = f32[256,768]{1,0:T(8,128)} fusion(bf16[4096,256]{1,0:T(8,128)(2,1)} %bitcast.89, bf16[4096,768]{0,1:T(8,128)(2,1)} %bitcast.87), kind=kOutput, calls=%fused_computation.113 | convolution fusion | flops 1610612736 | bytes 9175040 | tf_op jit(solution)/shard_map/th,td->hd/dot_general | solution.py:217
  179.2 7.5 %fusion.21 = f32[256,256]{1,0:T(8,128)} fusion(bf16[4096,256]{1,0:T(8,128)(2,1)S(1)} %bitcast.86, f32[4096,256]{1,0:T(8,128)} %fusion.10, bf16[4096,768]{0,1:T(8,128)(2,1)} %bitcast.88, bf16[256,768]{1,0:T(8,128)(2,1)} %param.18), kind=kOutput, calls=%fused_computation.29 | convolution fusion | flops 2149580800 | bytes 13238272 | tf_op jit(solution)/shard_map/tc,th->ch/dot_general | solution.py:218
  187.8 2.2 collective-permute-start.3
  191.7 4.2 collective-permute-done.2
  196.9 245.7 %all-reduce.5.cloned.1.call-done = (f32[256,256]{1,0:T(8,128)}, f32[256,768]{1,0:T(8,128)}) async-done(((f32[256,256]{1,0:T(8,128)}, f32[256,768]{1,0:T(8,128)}), (f32[256,256]{1,0:T(8,128)}, f32[256,768]{1,0:T(8,128)})) %all-reduce.5.cloned.1.call-update) | async-done | bytes 1048592 | tf_op jit(solution)/shard_map/psum | solution.py:224
  444.2 2.1 copy.68
  (88 shorter events, 26.9 us)
Async XLA Ops:
  7.2 48.6 %copy-start = (bf16[768,768]{1,0:T(8,128)(2,1)S(1)}, bf16[768,768]{1,0:T(8,128)(2,1)}, u32[]{:S(2)}) copy-start(bf16[768,768]{1,0:T(8,128)(2,1)} %param.19) | copy-start | bytes 3538948
  7.2 20.9 %copy-start.14 = (u32[256]{0:T(256)S(1)}, u32[256]{0:T(256)}, u32[]{:S(2)}) copy-start(u32[256]{0:T(256)} %constant.95) | copy-start | bytes 3076
  7.2 22.2 %copy-start.13 = (s32[16]{0:T(128)S(1)}, s32[16]{0:T(128)}, u32[]{:S(2)}) copy-start(s32[16]{0:T(128)} %param.14) | copy-start | bytes 196
  7.2 14.9 %copy-start.10 = (bf16[1,8,8,768]{3,2,1,0:T(8,128)(2,1)S(1)}, bf16[1,8,8,768]{3,2,1,0:T(8,128)(2,1)}, u32[]{:S(2)}) copy-start(bf16[1,8,8,768]{3,2,1,0:T(8,128)(2,1)} %param.16) | copy-start | bytes 294916
  7.2 48.6 %copy-start.6 = (bf16[1,8,8,768]{3,2,1,0:T(8,128)(2,1)S(1)}, bf16[1,8,8,768]{3,2,1,0:T(8,128)(2,1)}, u32[]{:S(2)}) copy-start(bf16[1,8,8,768]{3,2,1,0:T(8,128)(2,1)} %param.15) | copy-start | bytes 294916
  7.2 56.9 %copy-start.12 = (f32[8,768]{1,0:T(8,128)S(1)}, f32[8,768]{1,0:T(8,128)}, u32[]{:S(2)}) copy-start(f32[8,768]{1,0:T(8,128)} %param.21) | copy-start | bytes 73732
  14.6 56.8 %all-to-all-start = ((bf16[16,2,128,256]{3,2,1,0:T(8,128)(2,1)}), bf16[16,2,128,256]{3,2,1,0:T(8,128)(2,1)S(1)}, u32[]{:S(2)}, u32[]{:S(2)}) async-start(bf16[16,2,128,256]{3,2,1,0:T(8,128)(2,1)} %bitcast.5), calls=%async_computation | async-start | bytes 4194304 | tf_op jit(solution)/shard_map/all_to_all | solution.py:170
  22.1 420.5 %all-reduce.5.cloned.1.call-start = ((), (), s32[]{:S(2)}) async-start(), calls=%async_computation.1 | async-start | bytes 2097152 | tf_op jit(solution)/shard_map/psum | solution.py:224
  22.1 35.3 %collective-permute-start.5 = (bf16[1,8,768]{2,1,0:T(8,128)(2,1)S(1)}, bf16[1,8,768]{2,1,0:T(8,128)(2,1)S(1)}, u32[]{:S(2)}, u32[]{:S(2)}) collective-permute-start(bf16[1,8,768]{2,1,0:T(8,128)(2,1)S(1)} %get-tuple-element.48), channel_id=1, source_target_pairs={{32,0},{64,32},{96,64},{128,96},{160,128},{192,160},{224,192},{0,2... | collective-permute-start | bytes 36872 | tf_op jit(solution)/shard_map/ppermute | solution.py:24
  28.1 29.3 %collective-permute-start.4 = (bf16[1,8,768]{2,1,0:T(8,128)(2,1)S(1)}, bf16[1,8,768]{2,1,0:T(8,128)(2,1)S(1)}, u32[]{:S(2)}, u32[]{:S(2)}) collective-permute-start(bf16[1,8,768]{2,1,0:T(8,128)(2,1)S(1)} %get-tuple-element.47), channel_id=1, source_target_pairs={{0,32},{32,64},{64,96},{96,128},{128,160},{160,192},{192,224},{224... | collective-permute-start | bytes 36872 | tf_op jit(solution)/shard_map/ppermute | solution.py:21
  57.5 10.6 %collective-permute-start.7 = (bf16[10,1,768]{2,1,0:T(2,128)(2,1)S(1)}, bf16[10,1,768]{2,1,0:T(2,128)(2,1)S(1)}, u32[]{:S(2)}, u32[]{:S(2)}) collective-permute-start(bf16[10,1,768]{2,1,0:T(2,128)(2,1)S(1)} %get-tuple-element.44), channel_id=1, source_target_pairs={{2,0},{4,2},{6,4},{8,6},{10,8},{12,10},{14,12},{16,14},{18,16},{20... | collective-permute-start | bytes 46088 | tf_op jit(solution)/shard_map/ppermute | solution.py:24
  64.1 6.0 %collective-permute-start.6 = (bf16[10,1,768]{2,1,0:T(2,128)(2,1)S(1)}, bf16[10,1,768]{2,1,0:T(2,128)(2,1)S(1)}, u32[]{:S(2)}, u32[]{:S(2)}) collective-permute-start(bf16[10,1,768]{2,1,0:T(2,128)(2,1)S(1)} %get-tuple-element.43), channel_id=1, source_target_pairs={{0,2},{2,4},{4,6},{6,8},{8,10},{10,12},{12,14},{14,16},{16,18},{18... | collective-permute-start | bytes 46088 | tf_op jit(solution)/shard_map/ppermute | solution.py:21
  71.3 5.6 %copy-start.5 = (bf16[256,768]{1,0:T(8,128)(2,1)S(1)}, bf16[256,768]{1,0:T(8,128)(2,1)}, u32[]{:S(2)}) copy-start(bf16[256,768]{1,0:T(8,128)(2,1)} %param.18) | copy-start | bytes 1179652
  75.6 1.4 copy-start.4
  97.6 11.2 %copy-start.7 = (bf16[64,12,64]{0,2,1:T(8,128)(2,1)S(1)}, bf16[64,12,64]{0,2,1:T(8,128)(2,1)}, u32[]{:S(2)}) copy-start(bf16[64,12,64]{0,2,1:T(8,128)(2,1)} %copy.37) | copy-start | bytes 294916
  113.0 21.5 %copy-start.2 = (f32[12,64,4096]{2,1,0:T(8,128)}, f32[12,64,4096]{2,1,0:T(8,128)S(1)}, u32[]{:S(2)}) copy-start(f32[12,64,4096]{2,1,0:T(8,128)S(1)} %get-tuple-element.52) | copy-start | bytes 37748740
  113.1 7.3 %copy-start.3 = (bf16[4096,12,64]{0,2,1:T(8,128)(2,1)S(1)}, bf16[4096,12,64]{0,2,1:T(8,128)(2,1)}, u32[]{:S(2)}) copy-start(bf16[4096,12,64]{0,2,1:T(8,128)(2,1)} %reshape_reshape.11) | copy-start | bytes 18874372
  113.1 7.3 %copy-start.9 = (bf16[64,12,64]{2,1,0:T(8,128)(2,1)S(1)}, bf16[64,12,64]{2,1,0:T(8,128)(2,1)}, u32[]{:S(2)}) copy-start(bf16[64,12,64]{2,1,0:T(8,128)(2,1)} %copy-done.8) | copy-start | bytes 294916
  127.6 6.9 %copy-start.11 = (bf16[64,12,64]{0,2,1:T(8,128)(2,1)S(1)}, bf16[64,12,64]{0,2,1:T(8,128)(2,1)}, u32[]{:S(2)}) copy-start(bf16[64,12,64]{0,2,1:T(8,128)(2,1)} %copy.32) | copy-start | bytes 294916
  142.9 44.8 %collective-permute-start.1 = (bf16[1,8,768]{2,1,0:T(8,128)(2,1)S(1)}, bf16[1,8,768]{2,1,0:T(8,128)(2,1)S(1)}, u32[]{:S(2)}, u32[]{:S(2)}) collective-permute-start(bf16[1,8,768]{2,1,0:T(8,128)(2,1)S(1)} %get-tuple-element.46), channel_id=1, source_target_pairs={{32,0},{64,32},{96,64},{128,96},{160,128},{192,160},{224,192},{0,2... | collective-permute-start | bytes 36872 | tf_op jit(solution)/shard_map/ppermute | solution.py:24
  149.9 37.9 %collective-permute-start = (bf16[1,8,768]{2,1,0:T(8,128)(2,1)S(1)}, bf16[1,8,768]{2,1,0:T(8,128)(2,1)S(1)}, u32[]{:S(2)}, u32[]{:S(2)}) collective-permute-start(bf16[1,8,768]{2,1,0:T(8,128)(2,1)S(1)} %get-tuple-element.45), channel_id=1, source_target_pairs={{0,32},{32,64},{64,96},{96,128},{128,160},{160,192},{192,224},{224... | collective-permute-start | bytes 36872 | tf_op jit(solution)/shard_map/ppermute | solution.py:21
  179.2 267.1 %copy-start.1 = (bf16[768,768]{1,0:T(8,128)(2,1)S(1)}, bf16[768,768]{1,0:T(8,128)(2,1)}, u32[]{:S(2)}) copy-start(bf16[768,768]{1,0:T(8,128)(2,1)} %param.19) | copy-start | bytes 3538948
  187.8 4.0 collective-permute-start.3
  190.0 6.0 %collective-permute-start.2 = (bf16[10,1,768]{2,1,0:T(2,128)(2,1)S(1)}, bf16[10,1,768]{2,1,0:T(2,128)(2,1)S(1)}, u32[]{:S(2)}, u32[]{:S(2)}) collective-permute-start(bf16[10,1,768]{2,1,0:T(2,128)(2,1)S(1)} %get-tuple-element.41), channel_id=1, source_target_pairs={{0,2},{2,4},{4,6},{6,8},{8,10},{10,12},{12,14},{14,16},{16,18},{18... | collective-permute-start | bytes 46088 | tf_op jit(solution)/shard_map/ppermute | solution.py:21
  (1 other events, 0.7 us)
Sparse Core Ops, SparseCore 0:
  187.8 254.7 all-reduce.4
where the time goes:
time: 454 us; the launch traced here: 453 us
  waiting for transfers between devices  254 us (56%)
  matrix products  65.6 us (14%)
  local copies, waits for them, and re-layouts  49.6 us (11%)
  starting transfers between devices  28.4 us (6%)
  blocking collectives  22.9 us (5%)
  other arithmetic  17.9 us (4%)
  between operations  14.9 us (3%)
    psum x1, waiting for transfers between devices, per_device(): in_grad, out_grad = lax.psum((in_grad, out_grad), ('lat', 'lon', 'mem'))  246 us
    unnamed x1, blocking collectives  22.9 us
    ppermute x4, starting transfers between devices, extended(): lax.ppermute(lax.slice_in_dim(block, 0, width, axis=dim), axis, backward)  20.9 us
    dot_general x1, matrix products, mutual_attention_adjoint(): jnp.einsum('hqk,qhd->khd', logit_grad, query_heads, preferred_element_typ...  17.7 us
    convert_element_type x1, local copies, waits for them, and re-layouts, per_device(): obs_feat = jnp.dot(hidden_act, outer_perceptron_coeffs, preferred_element...  16.2 us
    another operation x1, local copies, waits for them, and re-layouts, mutual_attention_apply(): lookup_projection_entries.reshape(n_tokens, HEADS, CHANNELS_PER_ATT)  11.2 us
    unnamed x35, local copies, waits for them, and re-layouts  10.3 us
  transfers between devices with their start and end apart: 10, of which 4 were waited for; matrix products, arithmetic and copies ran while one was open for 11% of the time, Pallas kernels for 0%

commit v1 on v0

v1 whole, which is shorter than its diff:
```python
import math

import jax
import jax.numpy as jnp
from jax import lax
from jax.experimental import pallas as pl
from jax.experimental.pallas import tpu as pltpu
from jax.sharding import PartitionSpec as P

HEADS = 12
CHANNELS_PER_ATT = 64
GROUPS = 3
LANES = 256
CHUNK_BLOCKS = 4
MARK = 512.0


NEIGHBOURS = ((-1, -1), (-1, 0), (-1, 1), (0, -1), (0, 1), (1, -1), (1, 0), (1, 1))


def extended(block, sides, width):
    for axis, dim in sides:
        count = lax.axis_size(axis)
        forward = [(i, i + 1) for i in range(count - 1)]
        forward.append((count - 1, 0))
        backward = [(target, source) for source, target in forward]
        low = lax.ppermute(
            lax.slice_in_dim(block, block.shape[dim] - width, None, axis=dim), axis, forward
        )
        high = lax.ppermute(lax.slice_in_dim(block, 0, width, axis=dim), axis, backward)
        block = jnp.concatenate([low, block, high], axis=dim)
    return block


def mix_local(padded, keep_rows, adjacent_channel_coeffs, direction):
    values = padded.astype(jnp.float32) * keep_rows[:, None, None]
    n_rows = padded.shape[0] - 2
    n_cols = padded.shape[1] - 2
    total = values[1 : 1 + n_rows, 1 : 1 + n_cols]
    for offset_idx, (row_step, col_step) in enumerate(NEIGHBOURS):
        row_start = 1 + direction * row_step
        col_start = 1 + direction * col_step
        total = (
            total
            + adjacent_channel_coeffs[offset_idx]
            * values[row_start : row_start + n_rows, col_start : col_start + n_cols]
        )
    return total


def pack_kernel(target_ref, blocks_ref, send_ref, count_ref, mark_ref, sem):
    n_blocks = blocks_ref.shape[0]
    n_dest = send_ref.shape[0]
    cap = send_ref.shape[1]
    mark_ref[...] = jnp.full(mark_ref.shape, MARK, mark_ref.dtype)
    for d in range(n_dest):
        count_ref[d] = 0

    def copy_of(b, dest, slot):
        return pltpu.make_async_copy(blocks_ref.at[b], send_ref.at[dest, slot], sem.at[b])

    for b in range(n_blocks):
        dest = target_ref[b]
        slot = count_ref[dest]
        count_ref[dest] = slot + 1
        copy_of(b, dest, slot).start()

    def mark_of(d, slot):
        return pltpu.make_async_copy(
            mark_ref, send_ref.at[d, slot, pl.ds(0, mark_ref.shape[0])], sem.at[n_blocks + d * cap + slot]
        )

    for d in range(n_dest):
        for slot in range(cap):

            @pl.when(count_ref[d] <= slot)
            def _():
                mark_of(d, slot).start()

    for b in range(n_blocks):
        copy_of(b, 0, 0).wait()
    for d in range(n_dest):
        for slot in range(cap):

            @pl.when(count_ref[d] <= slot)
            def _():
                mark_of(d, slot).wait()


def pack_blocks(target_sector, blocks, n_dest, cap):
    n_blocks, block_len, width = blocks.shape
    return pl.pallas_call(
        pack_kernel,
        out_shape=jax.ShapeDtypeStruct((n_dest, cap, block_len, width), blocks.dtype),
        in_specs=[
            pl.BlockSpec(memory_space=pltpu.SMEM),
            pl.BlockSpec(memory_space=pl.ANY),
        ],
        out_specs=pl.BlockSpec(memory_space=pl.ANY),
        scratch_shapes=[
            pltpu.SMEM((n_dest,), jnp.int32),
            pltpu.VMEM((16, width), blocks.dtype),
            pltpu.SemaphoreType.DMA((n_blocks + n_dest * cap,)),
        ],
        name="pack_blocks",
    )(target_sector, blocks)


def block_mask():
    rows = lax.broadcasted_iota(jnp.int32, (LANES, LANES), 0) // CHANNELS_PER_ATT
    cols = lax.broadcasted_iota(jnp.int32, (LANES, LANES), 1) // CHANNELS_PER_ATT
    return rows == cols


def spread(values, group, mask):
    part = values[:, group * LANES : (group + 1) * LANES].astype(jnp.float32)
    return jnp.where(mask, jnp.concatenate([part] * (LANES // CHANNELS_PER_ATT), axis=0), 0.0)


def cells_kernel(cells_ref, grad_ref, probe_ref, outer_ref, qt_ref, gt_ref, xt_ref, gq_ref, self_ref, ot_ref):
    mask = block_mask()
    query = jnp.dot(cells_ref[...], probe_ref[...], preferred_element_type=jnp.float32)
    query = query.astype(jnp.bfloat16).astype(jnp.float32)
    cells = cells_ref[...].astype(jnp.float32)
    grad = grad_ref[...].astype(jnp.float32)
    for j in range(GROUPS):
        q_rows = spread(query, j, mask)
        g_rows = spread(grad, j, mask)
        gq_ref[j, 0:LANES] = g_rows.astype(jnp.bfloat16)
        gq_ref[j, LANES : 2 * LANES] = q_rows.astype(jnp.bfloat16)
        q_cols = q_rows.T
        g_cols = g_rows.T
        x_cols = spread(cells, j, mask).T
        qt_ref[j] = q_cols.astype(jnp.bfloat16)
        gt_ref[j] = g_cols.astype(jnp.bfloat16)
        xt_ref[j] = x_cols
        self_ref[0:1, j * LANES : (j + 1) * LANES] = jnp.sum(q_cols * x_cols, axis=0, keepdims=True)
        self_ref[1:2, j * LANES : (j + 1) * LANES] = jnp.sum(g_cols * x_cols, axis=0, keepdims=True)
        ot_ref[j * LANES : (j + 1) * LANES, :] = (
            outer_ref[:, j * LANES : (j + 1) * LANES].astype(jnp.float32).T.astype(jnp.bfloat16)
        )


def prepare_cells(cells, grad, probe, outer):
    width = cells.shape[1]
    hidden = outer.shape[0]
    return pl.pallas_call(
        cells_kernel,
        out_shape=(
            jax.ShapeDtypeStruct((GROUPS, LANES, LANES), jnp.bfloat16),
            jax.ShapeDtypeStruct((GROUPS, LANES, LANES), jnp.bfloat16),
            jax.ShapeDtypeStruct((GROUPS, LANES, LANES), jnp.float32),
            jax.ShapeDtypeStruct((GROUPS, 2 * LANES, LANES), jnp.bfloat16),
            jax.ShapeDtypeStruct((2, width), jnp.float32),
            jax.ShapeDtypeStruct((width, hidden), jnp.bfloat16),
        ),
        name="prepare_cells",
    )(cells, grad, probe, outer)


def contract_rows(left, right):
    return lax.dot_general(left, right, (((0,), (0,)), ((), ())), preferred_element_type=jnp.float32)


def tile_kernel(
    live_ref, recv_ref, qt_ref, gt_ref, xt_ref, gq_ref, self_ref, norm_ref, inner_ref, outer_ref, ot_ref,
    state_ref, grads_ref,
    x_s, f_s, p_s, d_s, h_s, m_s, l_s, peak_s, up_s, row_s, in_s, out_s, sem,
):
    n_src, cap, block_len, _ = recv_ref.shape
    n_slots = n_src * cap
    rows = CHUNK_BLOCKS * block_len
    f32 = jnp.float32
    bf16 = jnp.bfloat16

    def copy_in(src, slot, at):
        at_row = pl.multiple_of(at * block_len, block_len)
        return pltpu.make_async_copy(
            recv_ref.at[src, slot], x_s.at[pl.ds(at_row, block_len)], sem.at[at]
        )

    count = jnp.int32(0)
    for i in range(n_slots):
        live = live_ref[i]

        @pl.when(live > 0)
        def _(count=count, i=i):
            copy_in(i // cap, i % cap, count).start()

        count = count + live
    n_chunks = (count + CHUNK_BLOCKS - 1) // CHUNK_BLOCKS

    norm = norm_ref[...]
    self_score = self_ref[0:1, :] * norm
    m_s[...] = self_score
    l_s[...] = jnp.ones_like(l_s)
    up_s[...] = jnp.zeros_like(up_s)
    in_s[...] = jnp.zeros_like(in_s)
    out_s[...] = jnp.zeros_like(out_s)

    def forward(k, carry):
        for i in range(CHUNK_BLOCKS):
            at = k * CHUNK_BLOCKS + i

            @pl.when(at < count)
            def _():
                copy_in(0, 0, at).wait()

            @pl.when(at >= count)
            def _():
                at_row = pl.multiple_of(at * block_len, block_len)
                x_s[pl.ds(at_row, block_len), :] = jnp.zeros((block_len, x_s.shape[1]), bf16)

        start = pl.multiple_of(k * rows, rows)
        here = pl.ds(start, rows)
        pre = jnp.dot(x_s[here, :], inner_ref[...], preferred_element_type=f32)
        gate = 1.0 / (1.0 + jnp.exp(-pre))
        hidden = (pre * gate).astype(bf16)
        d_s[here, :] = gate * (1.0 + pre * (1.0 - gate))
        h_s[here, :] = hidden
        inside = lax.broadcasted_iota(jnp.int32, (rows, LANES), 0) < count * block_len - start
        for j in range(GROUPS):
            cols = pl.ds(j * LANES, LANES)
            feat = jnp.dot(hidden, outer_ref[:, cols], preferred_element_type=f32).astype(bf16)
            f_s[here, cols] = feat
            scores = jnp.dot(feat, qt_ref[j], preferred_element_type=f32) * norm[:, j * LANES : (j + 1) * LANES]
            scores = jnp.where(inside, scores, -jnp.inf)
            old = m_s[:, cols]
            peak = jnp.maximum(old, jnp.max(scores, axis=0, keepdims=True))
            fade = jnp.exp(old - peak)
            terms = jnp.exp(scores - peak)
            p_s[here, cols] = terms
            m_s[:, cols] = peak
            peak_s[k, :, cols] = peak
            l_s[:, cols] = l_s[:, cols] * fade + jnp.sum(terms, axis=0, keepdims=True)
            up_s[j] = up_s[j] * fade + contract_rows(feat, terms.astype(bf16))
        return carry

    lax.fori_loop(0, n_chunks, forward, 0)

    mask = block_mask()
    inverse = 1.0 / l_s[...]
    peak = m_s[...]
    self_prob = jnp.exp(self_score - peak) * inverse
    self_weight = self_prob.astype(bf16).astype(f32)
    for j in range(GROUPS):
        cols = slice(j * LANES, (j + 1) * LANES)
        update = jnp.where(mask, up_s[j] * inverse[:, cols], 0.0)
        row_s[:, cols] = (
            jnp.sum(update * gt_ref[j].astype(f32), axis=0, keepdims=True)
            + self_prob[:, cols] * self_ref[1:2, cols]
        )
        x_cols = xt_ref[j]
        state = (x_cols + (update + self_weight[:, cols] * x_cols)).T
        total = state[0:CHANNELS_PER_ATT]
        for h in range(1, LANES // CHANNELS_PER_ATT):
            total = total + state[h * CHANNELS_PER_ATT : (h + 1) * CHANNELS_PER_ATT]
        state_ref[:, cols] = total.astype(bf16)

    row_total = row_s[...]

    def backward(k, carry):
        start = pl.multiple_of(k * rows, rows)
        here = pl.ds(start, rows)
        scale = jnp.exp(peak_s[k] - peak) * inverse
        scaled = scale * norm
        hidden = h_s[here, :]
        hidden_grad = jnp.zeros((rows, LANES), f32)
        for j in range(GROUPS):
            cols = slice(j * LANES, (j + 1) * LANES)
            terms = p_s[here, cols]
            weights = (terms * scale[:, cols]).astype(bf16)
            weight_grad = jnp.dot(f_s[here, cols], gt_ref[j], preferred_element_type=f32)
            logit_grad = ((terms * scaled[:, cols]) * (weight_grad - row_total[:, cols])).astype(bf16)
            feat_grad = jnp.dot(
                jnp.concatenate([weights, logit_grad], axis=1), gq_ref[j], preferred_element_type=f32
            ).astype(bf16)
            hidden_grad = hidden_grad + jnp.dot(feat_grad, ot_ref[cols, :], preferred_element_type=f32)
            out_s[:, cols] = out_s[:, cols] + contract_rows(hidden, feat_grad)
        hidden_grad = (hidden_grad * d_s[here, :]).astype(bf16)
        in_s[...] = in_s[...] + contract_rows(x_s[here, :], hidden_grad)
        return carry

    lax.fori_loop(0, n_chunks, backward, 0)
    grads_ref[:, 0 : in_s.shape[1]] = in_s[...].astype(bf16)
    grads_ref[:, in_s.shape[1] :] = out_s[...].astype(bf16)


def tile_step(live, recv, qt, gt, xt, gq, self_dots, norm, inner, outer, ot, n_cells):
    n_src, cap, block_len, obs_width = recv.shape
    hidden, width = outer.shape
    n_slots = n_src * cap
    n_tokens = n_slots * block_len
    n_chunks = n_slots // CHUNK_BLOCKS
    vmem = pl.BlockSpec(memory_space=pltpu.VMEM)
    return pl.pallas_call(
        tile_kernel,
        out_shape=(
            jax.ShapeDtypeStruct((n_cells, width), jnp.bfloat16),
            jax.ShapeDtypeStruct((obs_width, hidden + width), jnp.bfloat16),
        ),
        in_specs=[pl.BlockSpec(memory_space=pltpu.SMEM), pl.BlockSpec(memory_space=pl.ANY)] + [vmem] * 9,
        out_specs=(vmem, vmem),
        scratch_shapes=[
            pltpu.VMEM((n_tokens, obs_width), jnp.bfloat16),
            pltpu.VMEM((n_tokens, width), jnp.bfloat16),
            pltpu.VMEM((n_tokens, width), jnp.float32),
            pltpu.VMEM((n_tokens, hidden), jnp.float32),
            pltpu.VMEM((n_tokens, hidden), jnp.bfloat16),
            pltpu.VMEM((1, width), jnp.float32),
            pltpu.VMEM((1, width), jnp.float32),
            pltpu.VMEM((n_chunks, 1, width), jnp.float32),
            pltpu.VMEM((GROUPS, LANES, LANES), jnp.float32),
            pltpu.VMEM((1, width), jnp.float32),
            pltpu.VMEM((obs_width, hidden), jnp.float32),
            pltpu.VMEM((hidden, width), jnp.float32),
            pltpu.SemaphoreType.DMA((n_slots,)),
        ],
        compiler_params=pltpu.CompilerParams(vmem_limit_bytes=50 * 1024 * 1024),
        name="tile_step",
    )(live, recv, qt, gt, xt, gq, self_dots, norm, inner, outer, ot)


def reduce_everywhere(grads):
    n_rows, n_cols = grads.shape
    ring = ("lon", "mem")
    count = lax.axis_size("lon") * lax.axis_size("mem")
    lat_count = lax.axis_size("lat")
    pieces = lax.all_to_all(
        grads.reshape(count, n_rows // count, n_cols), ring, split_axis=0, concat_axis=0, tiled=True
    )
    part = jnp.sum(pieces.astype(jnp.float32), axis=0)
    own = part.astype(jnp.bfloat16)
    parts = [own.astype(jnp.float32)]
    for shift in range(1, lat_count):
        pairs = [(i, (i + shift) % lat_count) for i in range(lat_count)]
        parts.append(lax.ppermute(own, "lat", pairs).astype(jnp.float32))
    while len(parts) > 1:
        half = len(parts) // 2
        parts = [parts[i] + parts[i + half] for i in range(half)]
    total = parts[0].astype(jnp.bfloat16)
    whole = lax.all_to_all(
        jnp.broadcast_to(total[None], (count,) + total.shape), ring, split_axis=0, concat_axis=0, tiled=True
    )
    return whole.reshape(n_rows, n_cols)


def per_device(
    measured_inputs,
    target_sector,
    hidden_member_fields,
    analysis_adjoint,
    inner_perceptron_coeffs,
    outer_perceptron_coeffs,
    probe_projector,
    logit_sharpness,
    adjacent_channel_coeffs,
):
    lon_count = lax.axis_size("lon")
    lat_count = lax.axis_size("lat")
    block_count = target_sector.shape[0]
    model_width = hidden_member_fields.shape[3]
    hidden_width = inner_perceptron_coeffs.shape[1]
    cell_rows = hidden_member_fields.shape[1]
    cell_cols = hidden_member_fields.shape[2]
    n_cells = cell_rows * cell_cols
    cap_slots = max(2, 2 * block_count // lon_count)
    send_blocks = pack_blocks(target_sector, measured_inputs, lon_count, cap_slots)
    obs_blocks = lax.all_to_all(send_blocks, "lon", split_axis=0, concat_axis=0, tiled=True)
    cot_padded = extended(analysis_adjoint[0], (("lat", 0), ("lon", 1)), 1)
    lat_index = lax.axis_index("lat")
    keep_rows = jnp.ones((cell_rows + 2,), jnp.float32)
    keep_rows = keep_rows.at[0].set(jnp.where(lat_index > 0, 1.0, 0.0))
    keep_rows = keep_rows.at[cell_rows + 1].set(jnp.where(lat_index < lat_count - 1, 1.0, 0.0))
    hidden_field_adjoint = (
        mix_local(cot_padded, keep_rows, adjacent_channel_coeffs, -1)
        .astype(jnp.bfloat16)
        .reshape(n_cells, model_width)
    )
    grid_point_entries = hidden_member_fields.reshape(n_cells, model_width)
    prepared = prepare_cells(
        grid_point_entries, hidden_field_adjoint, probe_projector, outer_perceptron_coeffs
    )
    qt, gt, xt, gq, self_dots, ot = prepared
    norm = jnp.repeat(logit_sharpness / math.sqrt(CHANNELS_PER_ATT), n_cells)[None, :]
    live = (obs_blocks[:, :, 0, 0] < MARK / 2).astype(jnp.int32).reshape(-1)
    revised_analysis, grads = tile_step(
        live, obs_blocks, qt, gt, xt, gq, self_dots, norm,
        inner_perceptron_coeffs, outer_perceptron_coeffs, ot, n_cells,
    )
    grads = reduce_everywhere(grads)
    state_grid = revised_analysis.reshape(cell_rows, cell_cols, model_width)
    state_padded = extended(state_grid, (("lat", 0), ("lon", 1)), 1)
    analysis = (
        mix_local(state_padded, keep_rows, adjacent_channel_coeffs, 1)
        .astype(jnp.bfloat16)
        .reshape(hidden_member_fields.shape)
    )
    grads = grads.astype(jnp.float32)
    return (analysis, grads[:, :hidden_width], grads[:, hidden_width:])


def solution(mesh):
    in_specs = (
        P(("lat", "lon", "mem"), None, None),
        P(("lat", "lon", "mem")),
        P("mem", "lat", "lon", None),
        P("mem", "lat", "lon", None),
        P(),
        P(),
        P(),
        P(),
        P(),
    )
    out_specs = (P("mem", "lat", "lon", None), P(), P())
    return jax.shard_map(
        per_device, mesh=mesh, in_specs=in_specs, out_specs=out_specs, check_vma=False
    )
```

time: 454 us -> 170 us (0.37)
  waiting for transfers between devices: 254 us -> 22.5 us
  matrix products: 65.6 us -> 0 us
  Pallas kernels: 0 us -> 54.3 us
  local copies, waits for them, and re-layouts: 49.6 us -> 9.41 us
  starting transfers between devices: 28.4 us -> 48.7 us
  other arithmetic: 17.9 us -> 2.8 us
  between operations: 14.9 us -> 0.82 us
  blocking collectives: 22.9 us -> 28.7 us
    psum x1 -> x0, waiting for transfers between devices: 246 us -> none  [per_device(): in_grad, out_grad = lax.psum((in_grad, out_grad), ('lat', 'lon', 'mem'))]
    dot_general x10 -> x0, matrix products: 65.6 us -> none  [the longest x1 17.7 us: mutual_attention_adjoint(): jnp.einsum('hqk,qhd->khd', logit_grad, query_heads, preferred_element_typ...]
    pallas_call x0 -> x3, Pallas kernels: none -> 54.3 us  [the longest x1 34 us: pack_blocks(): pl.pallas_call(pack_kernel, out_shape=jax.ShapeDtypeStruct((n_dest, cap,...]
    all_to_all x0 -> x1, blocking collectives: none -> 28.7 us  [reduce_everywhere(): lax.all_to_all(grads.reshape(count, n_rows // count, n_cols), ring, split...]
    unnamed x1 -> x0, blocking collectives: 22.9 us -> none
    ppermute x0 -> x7, starting transfers between devices: none -> 17.3 us  [reduce_everywhere(): parts.append(lax.ppermute(own, 'lat', pairs).astype(jnp.float32))]
    ppermute x4, waiting for transfers between devices: 6.27 us -> 22.5 us  [extended(): lax.ppermute(lax.slice_in_dim(block, block.shape[dim] - width, None, axis...]
    convert_element_type x1, local copies, waits for them, and re-layouts: 16.2 us -> 0.09 us  [per_device(): live = (obs_blocks[:, :, 0, 0] < MARK / 2).astype(jnp.int32).reshape(-1)]
  transfers between devices with their start and end apart: 10 -> 17, of which waited for: 4 -> 3; matrix products, arithmetic and copies ran while one was open for 11% -> 2% of each run, Pallas kernels for 0% -> 2%
where the time goes in v1:
time: 170 us; the launch traced here: 167 us
  Pallas kernels  54.3 us (32%)
  starting transfers between devices  48.7 us (29%)
  blocking collectives  28.7 us (17%)
  waiting for transfers between devices  22.5 us (13%)
  local copies, waits for them, and re-layouts  9.41 us (6%)
  other arithmetic  2.8 us (2%)
    pallas_call x1, Pallas kernels, pack_blocks(): pl.pallas_call(pack_kernel, out_shape=jax.ShapeDtypeStruct((n_dest, cap,...  34 us
    all_to_all x1, blocking collectives, reduce_everywhere(): lax.all_to_all(grads.reshape(count, n_rows // count, n_cols), ring, split...  28.7 us
    ppermute x4, waiting for transfers between devices, extended(): lax.ppermute(lax.slice_in_dim(block, block.shape[dim] - width, None, axis...  22.5 us
    ppermute x7, starting transfers between devices, reduce_everywhere(): parts.append(lax.ppermute(own, 'lat', pairs).astype(jnp.float32))  17.3 us
    pallas_call x1, Pallas kernels, tile_step(): pl.pallas_call(tile_kernel, out_shape=(jax.ShapeDtypeStruct((n_cells, wid...  16.8 us
    ppermute x4, starting transfers between devices, extended(): lax.ppermute(lax.slice_in_dim(block, 0, width, axis=dim), axis, backward)  11.3 us
    all_to_all x1, starting transfers between devices, per_device(): lax.all_to_all(send_blocks, 'lon', split_axis=0, concat_axis=0, tiled=True)  7.62 us
    ppermute x4, starting transfers between devices, extended(): lax.ppermute(lax.slice_in_dim(block, block.shape[dim] - width, None, axis...  7.01 us
  transfers between devices with their start and end apart: 17, of which 3 were waited for; matrix products, arithmetic and copies ran while one was open for 2% of the time, Pallas kernels for 2%

profile of v1, /device:TPU:2, one launch (start us, length us, event | category | flops | bytes accessed | tf_op | source)
XLA Modules:
  0.0 167.3 jit_solution(10129396663138329373)
XLA Ops:
  0.6 34.0 %pack_blocks.1 = bf16[16,2,128,256]{3,2,1,0:T(8,128)(2,1)} custom-call(s32[16]{0:T(128)} %target_ref.1, bf16[16,128,256]{2,1,0:T(8,128)(2,1)} %blocks_ref.1), custom_call_target="tpu_custom_call" | custom-call | tf_op jit(solution)/shard_map/pack_blocks/pallas_call | solution.py:92
  34.7 7.6 %all-to-all-start = ((bf16[16,2,128,256]{3,2,1,0:T(8,128)(2,1)}), bf16[16,2,128,256]{3,2,1,0:T(8,128)(2,1)S(1)}, u32[]{:S(2)}, u32[]{:S(2)}) async-start(bf16[16,2,128,256]{3,2,1,0:T(8,128)(2,1)} %pack_blocks.1), calls=%async_computation | async-start | bytes 4194304 | tf_op jit(solution)/shard_map/all_to_all | solution.py:369
  42.3 2.0 %collective-permute-start = (bf16[1,8,768]{2,1,0:T(8,128)(2,1)S(1)}, bf16[1,8,768]{2,1,0:T(8,128)(2,1)S(1)}, u32[]{:S(2)}, u32[]{:S(2)}) collective-permute-start(bf16[1,8,768]{2,1,0:T(8,128)(2,1)S(1)} %get-tuple-element.57), channel_id=1, source_target_pairs={{0,32},{32,64},{64,96},{96,128},{128,160},{160,192},{192,224},{224... | collective-permute-start | bytes 36872 | tf_op jit(solution)/shard_map/ppermute | solution.py:27
  44.3 4.1 %collective-permute-start.1 = (bf16[1,8,768]{2,1,0:T(8,128)(2,1)S(1)}, bf16[1,8,768]{2,1,0:T(8,128)(2,1)S(1)}, u32[]{:S(2)}, u32[]{:S(2)}) collective-permute-start(bf16[1,8,768]{2,1,0:T(8,128)(2,1)S(1)} %get-tuple-element.58), channel_id=1, source_target_pairs={{32,0},{64,32},{96,64},{128,96},{160,128},{192,160},{224,192},{0,2... | collective-permute-start | bytes 36872 | tf_op jit(solution)/shard_map/ppermute | solution.py:30
  48.4 1.6 collective-permute-done
  50.0 1.5 collective-permute-start.2
  51.6 2.7 %collective-permute-start.3 = (bf16[10,1,768]{2,1,0:T(2,128)(2,1)S(1)}, bf16[10,1,768]{2,1,0:T(2,128)(2,1)S(1)}, u32[]{:S(2)}, u32[]{:S(2)}) collective-permute-start(bf16[10,1,768]{2,1,0:T(2,128)(2,1)S(1)} %get-tuple-element.54), channel_id=1, source_target_pairs={{2,0},{4,2},{6,4},{8,6},{10,8},{12,10},{14,12},{16,14},{18,16},{20... | collective-permute-start | bytes 46088 | tf_op jit(solution)/shard_map/ppermute | solution.py:30
  54.5 14.7 %collective-permute-done.2 = bf16[10,1,768]{2,1,0:T(2,128)(2,1)S(1)} collective-permute-done((bf16[10,1,768]{2,1,0:T(2,128)(2,1)S(1)}, bf16[10,1,768]{2,1,0:T(2,128)(2,1)S(1)}, u32[]{:S(2)}, u32[]{:S(2)}) %collective-permute-start.2) | collective-permute-done | bytes 15392 | tf_op jit(solution)/shard_map/ppermute | solution.py:27
  70.2 3.5 %prepare_cells.1 = (bf16[3,256,256]{2,1,0:T(8,128)(2,1)}, bf16[3,256,256]{2,1,0:T(8,128)(2,1)}, f32[3,256,256]{2,1,0:T(8,128)}, bf16[3,512,256]{2,1,0:T(8,128)(2...) custom-call(bf16[64,768]{1,0:T(8,128)(2,1)} %bitcast.26, bf16[64,768]{1,0:T(8,128)(2,1)} %fusion.18.grad_ref, ...), custom_call_target="tpu_custom_call" | custom-call | tf_op jit(solution)/shard_map/prepare_cells/pallas_call | solution.py:147
  75.0 1.1 copy-done.1
  81.0 16.8 %tile_step.1 = (bf16[64,768]{1,0:T(8,128)(2,1)S(1)}, bf16[256,1024]{1,0:T(8,128)(2,1)S(1)}) custom-call(s32[32]{0:T(128)S(1)} %reshape.101.live_ref, bf16[16,2,128,256]{3,2,1,0:T(8,128)(2,1)} %copy-done.8, bf16[3,256,256]{2,1,0:T(8,128)(2,1)S(1)} %copy-done.3, bf16[3,256,256]{2,1,0:T(8,128)(2,1)S(1)} %copy-done.4, f32[3,256,256]{2,1,0:T(8,128)S(1)} %copy-done.1, ...), custom_call_target="tpu_custom_call" | custom-call | tf_op jit(solution)/shard_map/tile_step/pallas_call | solution.py:296
  97.8 28.7 %all_to_all.15 = bf16[32,8,1024]{2,1,0:T(8,128)(2,1)S(1)} all-to-all(bf16[32,8,1024]{2,1,0:T(8,128)(2,1)S(1)} %bitcast.21), channel_id=1, replica_groups=mesh['lat'=8,'lon'=16,'mem'=2] {'lon','mem'}, dimensions={0} | all-to-all | bytes 1048576 | tf_op jit(solution)/shard_map/all_to_all | solution.py:329
  126.6 2.7 %collective-permute-start.14 = (bf16[8,1024]{1,0:T(8,128)(2,1)S(1)}, bf16[8,1024]{1,0:T(8,128)(2,1)S(1)}, u32[]{:S(2)}, u32[]{:S(2)}) collective-permute-start(bf16[8,1024]{1,0:T(8,128)(2,1)S(1)} %reduce_sum.12), channel_id=1, source_target_pairs={{0,224},{32,0},{64,32},{96,64},{128,96},{160,128},{192,160},{224,1... | collective-permute-start | bytes 49160 | tf_op jit(solution)/shard_map/ppermute | solution.py:337
  129.3 3.4 %collective-permute-start.13 = (bf16[8,1024]{1,0:T(8,128)(2,1)S(1)}, bf16[8,1024]{1,0:T(8,128)(2,1)S(1)}, u32[]{:S(2)}, u32[]{:S(2)}) collective-permute-start(bf16[8,1024]{1,0:T(8,128)(2,1)S(1)} %reduce_sum.12), channel_id=1, source_target_pairs={{0,96},{32,128},{64,160},{96,192},{128,224},{160,0},{192,32},{224,... | collective-permute-start | bytes 49160 | tf_op jit(solution)/shard_map/ppermute | solution.py:337
  132.7 1.9 %collective-permute-start.12 = (bf16[8,1024]{1,0:T(8,128)(2,1)S(1)}, bf16[8,1024]{1,0:T(8,128)(2,1)S(1)}, u32[]{:S(2)}, u32[]{:S(2)}) collective-permute-start(bf16[8,1024]{1,0:T(8,128)(2,1)S(1)} %reduce_sum.12), channel_id=1, source_target_pairs={{0,160},{32,192},{64,224},{96,0},{128,32},{160,64},{192,96},{224,1... | collective-permute-start | bytes 49160 | tf_op jit(solution)/shard_map/ppermute | solution.py:337
  134.6 1.8 %collective-permute-start.11 = (bf16[8,1024]{1,0:T(8,128)(2,1)S(1)}, bf16[8,1024]{1,0:T(8,128)(2,1)S(1)}, u32[]{:S(2)}, u32[]{:S(2)}) collective-permute-start(bf16[8,1024]{1,0:T(8,128)(2,1)S(1)} %reduce_sum.12), channel_id=1, source_target_pairs={{0,32},{32,64},{64,96},{96,128},{128,160},{160,192},{192,224},{224... | collective-permute-start | bytes 49160 | tf_op jit(solution)/shard_map/ppermute | solution.py:337
  136.4 3.6 %collective-permute-start.10 = (bf16[8,1024]{1,0:T(8,128)(2,1)S(1)}, bf16[8,1024]{1,0:T(8,128)(2,1)S(1)}, u32[]{:S(2)}, u32[]{:S(2)}) collective-permute-start(bf16[8,1024]{1,0:T(8,128)(2,1)S(1)} %reduce_sum.12), channel_id=1, source_target_pairs={{0,192},{32,224},{64,0},{96,32},{128,64},{160,96},{192,128},{224,1... | collective-permute-start | bytes 49160 | tf_op jit(solution)/shard_map/ppermute | solution.py:337
  140.0 3.9 %collective-permute-start.8 = (bf16[8,1024]{1,0:T(8,128)(2,1)S(1)}, bf16[8,1024]{1,0:T(8,128)(2,1)S(1)}, u32[]{:S(2)}, u32[]{:S(2)}) collective-permute-start(bf16[8,1024]{1,0:T(8,128)(2,1)S(1)} %reduce_sum.12), channel_id=1, source_target_pairs={{0,128},{32,160},{64,192},{96,224},{128,0},{160,32},{192,64},{224,... | collective-permute-start | bytes 49160 | tf_op jit(solution)/shard_map/ppermute | solution.py:337
  143.9 1.9 %collective-permute-start.4 = (bf16[1,8,768]{2,1,0:T(8,128)(2,1)S(1)}, bf16[1,8,768]{2,1,0:T(8,128)(2,1)S(1)}, u32[]{:S(2)}, u32[]{:S(2)}) collective-permute-start(bf16[1,8,768]{2,1,0:T(8,128)(2,1)S(1)} %get-tuple-element.55), channel_id=1, source_target_pairs={{0,32},{32,64},{64,96},{96,128},{128,160},{160,192},{192,224},{224... | collective-permute-start | bytes 36872 | tf_op jit(solution)/shard_map/ppermute | solution.py:27
  145.9 1.9 %collective-permute-start.5 = (bf16[1,8,768]{2,1,0:T(8,128)(2,1)S(1)}, bf16[1,8,768]{2,1,0:T(8,128)(2,1)S(1)}, u32[]{:S(2)}, u32[]{:S(2)}) collective-permute-start(bf16[1,8,768]{2,1,0:T(8,128)(2,1)S(1)} %get-tuple-element.56), channel_id=1, source_target_pairs={{32,0},{64,32},{96,64},{128,96},{160,128},{192,160},{224,192},{0,2... | collective-permute-start | bytes 36872 | tf_op jit(solution)/shard_map/ppermute | solution.py:30
  148.7 5.4 %all-to-all-start.2 = ((bf16[32,8,1024]{2,1,0:T(8,128)(2,1)}), bf16[32,8,1024]{2,1,0:T(8,128)(2,1)S(1)}, u32[]{:S(2)}, u32[]{:S(2)}) async-start(bf16[32,8,1024]{2,1,0:T(8,128)(2,1)} %broadcast_in_dim.5), calls=%async_computation.2 | async-start | bytes 1048576 | tf_op jit(solution)/shard_map/all_to_all | solution.py:342
  154.2 1.5 collective-permute-start.6
  155.7 2.7 %collective-permute-start.7 = (bf16[10,1,768]{2,1,0:T(2,128)(2,1)S(1)}, bf16[10,1,768]{2,1,0:T(2,128)(2,1)S(1)}, u32[]{:S(2)}, u32[]{:S(2)}) collective-permute-start(bf16[10,1,768]{2,1,0:T(2,128)(2,1)S(1)} %get-tuple-element.52), channel_id=1, source_target_pairs={{2,0},{4,2},{6,4},{8,6},{10,8},{12,10},{14,12},{16,14},{18,16},{20... | collective-permute-start | bytes 46088 | tf_op jit(solution)/shard_map/ppermute | solution.py:30
  158.4 6.2 %collective-permute-done.6 = bf16[10,1,768]{2,1,0:T(2,128)(2,1)S(1)} collective-permute-done((bf16[10,1,768]{2,1,0:T(2,128)(2,1)S(1)}, bf16[10,1,768]{2,1,0:T(2,128)(2,1)S(1)}, u32[]{:S(2)}, u32[]{:S(2)}) %collective-permute-start.6) | collective-permute-done | bytes 15392 | tf_op jit(solution)/shard_map/ppermute | solution.py:27
  (60 shorter events, 11.1 us)
Async XLA Ops:
  34.7 7.7 %copy-start.9 = (bf16[1,8,8,768]{3,2,1,0:T(8,128)(2,1)S(1)}, bf16[1,8,8,768]{3,2,1,0:T(8,128)(2,1)}, u32[]{:S(2)}) copy-start(bf16[1,8,8,768]{3,2,1,0:T(8,128)(2,1)} %param.16) | copy-start | bytes 294916
  34.7 13.7 %copy-start.11 = (f32[12]{0:T(128)S(1)}, f32[12]{0:T(128)}, u32[]{:S(2)}) copy-start(f32[12]{0:T(128)} %param.20) | copy-start | bytes 148
  34.7 19.6 %copy-start.10 = (f32[8,768]{1,0:T(8,128)S(1)}, f32[8,768]{1,0:T(8,128)}, u32[]{:S(2)}) copy-start(f32[8,768]{1,0:T(8,128)} %param.21) | copy-start | bytes 73732
  34.7 39.0 %all-to-all-start = ((bf16[16,2,128,256]{3,2,1,0:T(8,128)(2,1)}), bf16[16,2,128,256]{3,2,1,0:T(8,128)(2,1)S(1)}, u32[]{:S(2)}, u32[]{:S(2)}) async-start(bf16[16,2,128,256]{3,2,1,0:T(8,128)(2,1)} %pack_blocks.1), calls=%async_computation | async-start | bytes 4194304 | tf_op jit(solution)/shard_map/all_to_all | solution.py:369
  42.3 7.6 %collective-permute-start = (bf16[1,8,768]{2,1,0:T(8,128)(2,1)S(1)}, bf16[1,8,768]{2,1,0:T(8,128)(2,1)S(1)}, u32[]{:S(2)}, u32[]{:S(2)}) collective-permute-start(bf16[1,8,768]{2,1,0:T(8,128)(2,1)S(1)} %get-tuple-element.57), channel_id=1, source_target_pairs={{0,32},{32,64},{64,96},{96,128},{128,160},{160,192},{192,224},{224... | collective-permute-start | bytes 36872 | tf_op jit(solution)/shard_map/ppermute | solution.py:27
  44.3 5.6 %collective-permute-start.1 = (bf16[1,8,768]{2,1,0:T(8,128)(2,1)S(1)}, bf16[1,8,768]{2,1,0:T(8,128)(2,1)S(1)}, u32[]{:S(2)}, u32[]{:S(2)}) collective-permute-start(bf16[1,8,768]{2,1,0:T(8,128)(2,1)S(1)} %get-tuple-element.58), channel_id=1, source_target_pairs={{32,0},{64,32},{96,64},{128,96},{160,128},{192,160},{224,192},{0,2... | collective-permute-start | bytes 36872 | tf_op jit(solution)/shard_map/ppermute | solution.py:30
  50.0 19.2 %collective-permute-start.2 = (bf16[10,1,768]{2,1,0:T(2,128)(2,1)S(1)}, bf16[10,1,768]{2,1,0:T(2,128)(2,1)S(1)}, u32[]{:S(2)}, u32[]{:S(2)}) collective-permute-start(bf16[10,1,768]{2,1,0:T(2,128)(2,1)S(1)} %get-tuple-element.53), channel_id=1, source_target_pairs={{0,2},{2,4},{4,6},{6,8},{8,10},{10,12},{12,14},{14,16},{16,18},{18... | collective-permute-start | bytes 46088 | tf_op jit(solution)/shard_map/ppermute | solution.py:27
  51.6 17.7 %collective-permute-start.3 = (bf16[10,1,768]{2,1,0:T(2,128)(2,1)S(1)}, bf16[10,1,768]{2,1,0:T(2,128)(2,1)S(1)}, u32[]{:S(2)}, u32[]{:S(2)}) collective-permute-start(bf16[10,1,768]{2,1,0:T(2,128)(2,1)S(1)} %get-tuple-element.54), channel_id=1, source_target_pairs={{2,0},{4,2},{6,4},{8,6},{10,8},{12,10},{14,12},{16,14},{18,16},{20... | collective-permute-start | bytes 46088 | tf_op jit(solution)/shard_map/ppermute | solution.py:30
  54.5 20.5 %copy-start = (bf16[256,768]{1,0:T(8,128)(2,1)S(1)}, bf16[256,768]{1,0:T(8,128)(2,1)}, u32[]{:S(2)}) copy-start(bf16[256,768]{1,0:T(8,128)(2,1)} %outer_ref.3) | copy-start | bytes 1179652
  54.5 20.5 %copy-start.6 = (bf16[256,256]{1,0:T(8,128)(2,1)S(1)}, bf16[256,256]{1,0:T(8,128)(2,1)}, u32[]{:S(2)}) copy-start(bf16[256,256]{1,0:T(8,128)(2,1)} %inner_ref.1) | copy-start | bytes 393220
  73.7 1.3 copy-start.8
  75.0 1.1 copy-start.1
  126.6 13.4 %collective-permute-start.14 = (bf16[8,1024]{1,0:T(8,128)(2,1)S(1)}, bf16[8,1024]{1,0:T(8,128)(2,1)S(1)}, u32[]{:S(2)}, u32[]{:S(2)}) collective-permute-start(bf16[8,1024]{1,0:T(8,128)(2,1)S(1)} %reduce_sum.12), channel_id=1, source_target_pairs={{0,224},{32,0},{64,32},{96,64},{128,96},{160,128},{192,160},{224,1... | collective-permute-start | bytes 49160 | tf_op jit(solution)/shard_map/ppermute | solution.py:337
  129.3 10.7 %collective-permute-start.13 = (bf16[8,1024]{1,0:T(8,128)(2,1)S(1)}, bf16[8,1024]{1,0:T(8,128)(2,1)S(1)}, u32[]{:S(2)}, u32[]{:S(2)}) collective-permute-start(bf16[8,1024]{1,0:T(8,128)(2,1)S(1)} %reduce_sum.12), channel_id=1, source_target_pairs={{0,96},{32,128},{64,160},{96,192},{128,224},{160,0},{192,32},{224,... | collective-permute-start | bytes 49160 | tf_op jit(solution)/shard_map/ppermute | solution.py:337
  132.7 11.2 %collective-permute-start.12 = (bf16[8,1024]{1,0:T(8,128)(2,1)S(1)}, bf16[8,1024]{1,0:T(8,128)(2,1)S(1)}, u32[]{:S(2)}, u32[]{:S(2)}) collective-permute-start(bf16[8,1024]{1,0:T(8,128)(2,1)S(1)} %reduce_sum.12), channel_id=1, source_target_pairs={{0,160},{32,192},{64,224},{96,0},{128,32},{160,64},{192,96},{224,1... | collective-permute-start | bytes 49160 | tf_op jit(solution)/shard_map/ppermute | solution.py:337
  134.6 11.3 %collective-permute-start.11 = (bf16[8,1024]{1,0:T(8,128)(2,1)S(1)}, bf16[8,1024]{1,0:T(8,128)(2,1)S(1)}, u32[]{:S(2)}, u32[]{:S(2)}) collective-permute-start(bf16[8,1024]{1,0:T(8,128)(2,1)S(1)} %reduce_sum.12), channel_id=1, source_target_pairs={{0,32},{32,64},{64,96},{96,128},{128,160},{160,192},{192,224},{224... | collective-permute-start | bytes 49160 | tf_op jit(solution)/shard_map/ppermute | solution.py:337
  136.4 11.4 %collective-permute-start.10 = (bf16[8,1024]{1,0:T(8,128)(2,1)S(1)}, bf16[8,1024]{1,0:T(8,128)(2,1)S(1)}, u32[]{:S(2)}, u32[]{:S(2)}) collective-permute-start(bf16[8,1024]{1,0:T(8,128)(2,1)S(1)} %reduce_sum.12), channel_id=1, source_target_pairs={{0,192},{32,224},{64,0},{96,32},{128,64},{160,96},{192,128},{224,1... | collective-permute-start | bytes 49160 | tf_op jit(solution)/shard_map/ppermute | solution.py:337
  140.0 7.8 %collective-permute-start.9 = (bf16[8,1024]{1,0:T(8,128)(2,1)S(1)}, bf16[8,1024]{1,0:T(8,128)(2,1)S(1)}, u32[]{:S(2)}, u32[]{:S(2)}) collective-permute-start(bf16[8,1024]{1,0:T(8,128)(2,1)S(1)} %reduce_sum.12), channel_id=1, source_target_pairs={{0,64},{32,96},{64,128},{96,160},{128,192},{160,224},{192,0},{224,... | collective-permute-start | bytes 49160 | tf_op jit(solution)/shard_map/ppermute | solution.py:337
  140.0 7.8 %collective-permute-start.8 = (bf16[8,1024]{1,0:T(8,128)(2,1)S(1)}, bf16[8,1024]{1,0:T(8,128)(2,1)S(1)}, u32[]{:S(2)}, u32[]{:S(2)}) collective-permute-start(bf16[8,1024]{1,0:T(8,128)(2,1)S(1)} %reduce_sum.12), channel_id=1, source_target_pairs={{0,128},{32,160},{64,192},{96,224},{128,0},{160,32},{192,64},{224,... | collective-permute-start | bytes 49160 | tf_op jit(solution)/shard_map/ppermute | solution.py:337
  143.9 10.2 %collective-permute-start.4 = (bf16[1,8,768]{2,1,0:T(8,128)(2,1)S(1)}, bf16[1,8,768]{2,1,0:T(8,128)(2,1)S(1)}, u32[]{:S(2)}, u32[]{:S(2)}) collective-permute-start(bf16[1,8,768]{2,1,0:T(8,128)(2,1)S(1)} %get-tuple-element.55), channel_id=1, source_target_pairs={{0,32},{32,64},{64,96},{96,128},{128,160},{160,192},{192,224},{224... | collective-permute-start | bytes 36872 | tf_op jit(solution)/shard_map/ppermute | solution.py:27
  145.9 8.3 %collective-permute-start.5 = (bf16[1,8,768]{2,1,0:T(8,128)(2,1)S(1)}, bf16[1,8,768]{2,1,0:T(8,128)(2,1)S(1)}, u32[]{:S(2)}, u32[]{:S(2)}) collective-permute-start(bf16[1,8,768]{2,1,0:T(8,128)(2,1)S(1)} %get-tuple-element.56), channel_id=1, source_target_pairs={{32,0},{64,32},{96,64},{128,96},{160,128},{192,160},{224,192},{0,2... | collective-permute-start | bytes 36872 | tf_op jit(solution)/shard_map/ppermute | solution.py:30
  148.7 16.8 %all-to-all-start.2 = ((bf16[32,8,1024]{2,1,0:T(8,128)(2,1)}), bf16[32,8,1024]{2,1,0:T(8,128)(2,1)S(1)}, u32[]{:S(2)}, u32[]{:S(2)}) async-start(bf16[32,8,1024]{2,1,0:T(8,128)(2,1)} %broadcast_in_dim.5), calls=%async_computation.2 | async-start | bytes 1048576 | tf_op jit(solution)/shard_map/all_to_all | solution.py:342
  154.2 10.4 %collective-permute-start.6 = (bf16[10,1,768]{2,1,0:T(2,128)(2,1)S(1)}, bf16[10,1,768]{2,1,0:T(2,128)(2,1)S(1)}, u32[]{:S(2)}, u32[]{:S(2)}) collective-permute-start(bf16[10,1,768]{2,1,0:T(2,128)(2,1)S(1)} %get-tuple-element.51), channel_id=1, source_target_pairs={{0,2},{2,4},{4,6},{6,8},{8,10},{10,12},{12,14},{14,16},{16,18},{18... | collective-permute-start | bytes 46088 | tf_op jit(solution)/shard_map/ppermute | solution.py:27
  155.7 8.9 %collective-permute-start.7 = (bf16[10,1,768]{2,1,0:T(2,128)(2,1)S(1)}, bf16[10,1,768]{2,1,0:T(2,128)(2,1)S(1)}, u32[]{:S(2)}, u32[]{:S(2)}) collective-permute-start(bf16[10,1,768]{2,1,0:T(2,128)(2,1)S(1)} %get-tuple-element.52), channel_id=1, source_target_pairs={{2,0},{4,2},{6,4},{8,6},{10,8},{12,10},{14,12},{16,14},{18,16},{20... | collective-permute-start | bytes 46088 | tf_op jit(solution)/shard_map/ppermute | solution.py:30
  (5 other events, 4.8 us)
